TPU v7x, 32 devices: a whole 2x2x4 slice. The times are simulated.
32 devices in a mesh: seq: 8 (over z, y), tensor: 4 (over x, core).
Axes of the slice: x: 2, y: 2, z: 4, core: 2. Of those that a mesh axis runs over, the one named last changes fastest.
Arguments:
- inputs: bfloat16 [1024, 3, 4096], P('seq', None, 'tensor'), may hold values from -6 to 6
- short_taps: float32 [7, 3, 4096], P(None, None, 'tensor'), may hold values from -2 to 2
- medium_taps: float32 [120, 4096], P(None, 'tensor'), may hold values from -0.5 to 0.5
- long_filter: float32 [1024, 4096], P('seq', 'tensor'), may hold values from -4 to 4
- out_weight: bfloat16 [8192, 4096], P(None, 'tensor'), may hold values from -0.09375 to 0.09375
- out_cotangent: bfloat16 [1024, 8192], P('seq', 'tensor'), may hold values from -6 to 6
Outputs:
- output: bfloat16 [1024, 8192], P('seq', 'tensor')
- input_grad: bfloat16 [1024, 3, 4096], P('seq', None, 'tensor')
- filter_grad: float32 [1024, 4096], P('seq', 'tensor')
- medium_grad: float32 [120, 4096], P(None, 'tensor')
- short_grad: float32 [7, 3, 4096], P(None, None, 'tensor')
All inputs are finite; a program needn't handle non-finite values.
Results may differ from a plain program's by a relative error of at most 0.013.
Values may be sent and summed in bfloat16 or wider, within the bound.
No kernel may reach another device: no remote copies, remote signals or barrier semaphores. Data moves between devices by JAX's collectives and lax.ppermute only.
A program may use at most 128 MiB of HBM per device.

v0:
```python
import math
import jax
import jax.numpy as jnp
from jax import lax
from jax.sharding import PartitionSpec as P

precise = lax.Precision.HIGHEST


def from_behind(value, axis, steps):
    count = lax.axis_size(axis)
    leading, last = (max(0, -steps), min(count, count - steps))
    return lax.ppermute(value, axis, [(source, source + steps) for source in range(leading, last)])


def as_sent(shard):

    def short(part):
        return part.astype(jnp.bfloat16) if part.dtype == jnp.float32 else part

    return jax.tree.map(short, shard)


def correlate(signal, kernel):
    channels = kernel.shape[1]
    result = lax.conv_general_dilated(
        signal[None],
        kernel[:, None, :],
        (1,),
        "VALID",
        dimension_numbers=("NWC", "WIO", "NWC"),
        feature_group_count=channels,
        precision=precise,
    )
    return result[0]


def angles(left_index, right_index, modulus):
    return (left_index * right_index % modulus).astype(jnp.float32) * (2.0 * math.pi / modulus)


def to_spectrum(signals, cos_table, sin_table):
    signal_count = signals.shape[0]
    length = signals.shape[1]
    channels = signals.shape[2]
    devices = lax.axis_size("seq")
    position = lax.axis_index("seq")
    stride = length // devices
    modulus = 2 * devices * length
    columns = lax.all_to_all(
        signals.reshape(signal_count, devices, stride, channels),
        "seq",
        split_axis=1,
        concat_axis=1,
        tiled=True,
    )
    coarse = jnp.arange(2 * devices, dtype=jnp.int32)
    sources = jnp.arange(devices, dtype=jnp.int32)
    coarse_angle = angles(coarse[:, None], sources[None, :], 2 * devices)
    first_real = jnp.einsum("kp,spmc->skmc", jnp.cos(coarse_angle), columns, precision=precise)
    first_imag = -jnp.einsum("kp,spmc->skmc", jnp.sin(coarse_angle), columns, precision=precise)
    local_rows = position * stride + jnp.arange(stride, dtype=jnp.int32)
    twiddle = angles(coarse[:, None], local_rows[None, :], modulus)
    cosine_values = jnp.cos(twiddle)[None, :, :, None]
    sine_part = jnp.sin(twiddle)[None, :, :, None]
    turned = jnp.stack(
        [
            first_real * cosine_values + first_imag * sine_part,
            first_imag * cosine_values - first_real * sine_part,
        ]
    )
    arrived = lax.all_to_all(turned, "seq", split_axis=2, concat_axis=3, tiled=True)
    spec_real = jnp.einsum("km,sjmc->sjkc", cos_table, arrived[0], precision=precise) + jnp.einsum(
        "km,sjmc->sjkc", sin_table, arrived[1], precision=precise
    )
    spec_imag = jnp.einsum("km,sjmc->sjkc", cos_table, arrived[1], precision=precise) - jnp.einsum(
        "km,sjmc->sjkc", sin_table, arrived[0], precision=precise
    )
    return (spec_real, spec_imag)


def from_spectrum(spec_real, spec_imag, cos_table, sin_table):
    signal_count = spec_real.shape[0]
    length = spec_real.shape[2]
    channels = spec_real.shape[3]
    devices = lax.axis_size("seq")
    position = lax.axis_index("seq")
    modulus = 2 * devices * length
    fine_real = jnp.einsum("mk,sjkc->sjmc", cos_table, spec_real, precision=precise) - jnp.einsum(
        "mk,sjkc->sjmc", sin_table, spec_imag, precision=precise
    )
    fine_imag = jnp.einsum("mk,sjkc->sjmc", cos_table, spec_imag, precision=precise) + jnp.einsum(
        "mk,sjkc->sjmc", sin_table, spec_real, precision=precise
    )
    held = 2 * position + jnp.arange(2, dtype=jnp.int32)
    all_rows = jnp.arange(length, dtype=jnp.int32)
    twiddle = angles(held[:, None], all_rows[None, :], modulus)
    cosine_values = jnp.cos(twiddle)[None, :, :, None]
    sine_part = jnp.sin(twiddle)[None, :, :, None]
    turned = jnp.stack(
        [
            fine_real * cosine_values - fine_imag * sine_part,
            fine_real * sine_part + fine_imag * cosine_values,
        ]
    )
    arrived = lax.all_to_all(turned, "seq", split_axis=3, concat_axis=2, tiled=True)
    coarse = jnp.arange(2 * devices, dtype=jnp.int32)
    sources = jnp.arange(devices, dtype=jnp.int32)
    coarse_angle = angles(sources[:, None], coarse[None, :], 2 * devices)
    blocks = (
        jnp.einsum("pk,skmc->spmc", jnp.cos(coarse_angle), arrived[0], precision=precise)
        - jnp.einsum("pk,skmc->spmc", jnp.sin(coarse_angle), arrived[1], precision=precise)
    ) / modulus
    returned = lax.all_to_all(blocks, "seq", split_axis=1, concat_axis=1, tiled=True)
    return returned.reshape(signal_count, length, channels)


def local(inputs, short_taps, medium_taps, long_filter, out_weight, out_cotangent):
    length = inputs.shape[0]
    groups = inputs.shape[1]
    channels = inputs.shape[2]
    short_reach = short_taps.shape[0]
    medium_reach = medium_taps.shape[0]
    devices = lax.axis_size("seq")
    scale = 1.0 / math.sqrt(length * devices)
    flat_inputs = inputs.reshape(length, groups * channels)
    short_flat = short_taps.reshape(short_reach, groups * channels)
    input_edge = from_behind(flat_inputs[length - (short_reach - 1) :], "seq", 1)
    extended_inputs = jnp.concatenate([input_edge, flat_inputs], 0).astype(jnp.float32)
    featured = correlate(extended_inputs, short_flat[::-1])
    gated = featured[:, channels : 2 * channels] * featured[:, 2 * channels :]
    gated_edge = from_behind(as_sent(gated[length - (medium_reach - 1) :]), "seq", 1)
    extended_gated = jnp.concatenate([gated_edge, gated], 0)
    query_branch = featured[:, :channels]
    key_branch = featured[:, channels : 2 * channels]
    value_branch = featured[:, 2 * channels :]
    mixed = correlate(extended_gated, medium_taps[::-1])
    all_rows = jnp.arange(length, dtype=jnp.int32)
    grid_angle = angles(all_rows[:, None], all_rows[None, :], length)
    cos_table = jnp.cos(grid_angle)
    sin_table = jnp.sin(grid_angle)
    spec_real, spec_imag = to_spectrum(jnp.stack([mixed, long_filter]), cos_table, sin_table)
    mixed_real = spec_real[0]
    mixed_imag = spec_imag[0]
    filter_real = spec_real[1]
    filter_imag = spec_imag[1]
    conv_real = mixed_real * filter_real - mixed_imag * filter_imag
    conv_imag = mixed_real * filter_imag + mixed_imag * filter_real
    convolved = from_spectrum(conv_real[None], conv_imag[None], cos_table, sin_table)[0]
    product = (query_branch * convolved).astype(jnp.bfloat16)
    partial_out = lax.dot_general(
        product, out_weight, (((1,), (1,)), ((), ())), preferred_element_type=jnp.float32
    )
    output = lax.psum_scatter(partial_out, "tensor", scatter_dimension=1, tiled=True).astype(
        jnp.bfloat16
    )
    full_cotangent = lax.all_gather(out_cotangent, "tensor", axis=1, tiled=True)
    product_grad = jnp.dot(full_cotangent, out_weight, preferred_element_type=jnp.float32)
    query_grad = product_grad * convolved
    convolved_grad = product_grad * query_branch
    grad_real, grad_imag = to_spectrum(convolved_grad[None], cos_table, sin_table)
    grad_real = grad_real[0]
    grad_imag = grad_imag[0]
    back_real = jnp.stack(
        [
            filter_real * grad_real + filter_imag * grad_imag,
            mixed_real * grad_real + mixed_imag * grad_imag,
        ]
    )
    back_imag = jnp.stack(
        [
            filter_real * grad_imag - filter_imag * grad_real,
            mixed_real * grad_imag - mixed_imag * grad_real,
        ]
    )
    timed = from_spectrum(back_real, back_imag, cos_table, sin_table)
    mixed_grad = timed[0]
    filter_grad = timed[1] * scale
    mixed_edge = from_behind(as_sent(mixed_grad[: medium_reach - 1]), "seq", -1)
    gated_grad = correlate(jnp.concatenate([mixed_grad, mixed_edge], 0), medium_taps)
    medium_part = correlate(extended_gated, mixed_grad)[::-1]
    feature_gradient = jnp.concatenate(
        [query_grad, gated_grad * value_branch, gated_grad * key_branch], 1
    )
    featured_edge = from_behind(as_sent(feature_gradient[: short_reach - 1]), "seq", -1)
    input_grad = (
        correlate(jnp.concatenate([feature_gradient, featured_edge], 0), short_flat)
        .astype(jnp.bfloat16)
        .reshape(length, groups, channels)
    )
    short_part = correlate(extended_inputs, feature_gradient)[::-1]
    medium_sum, short_sum = (
        lax.psum(medium_part.astype(jnp.bfloat16), "seq").astype(jnp.float32),
        lax.psum(short_part.astype(jnp.bfloat16), "seq").astype(jnp.float32),
    )
    medium_grad = medium_sum * scale
    short_grad = (short_sum * scale).reshape(short_reach, groups, channels)
    return (output, input_grad, filter_grad, medium_grad, short_grad)


def solution(mesh):
    return jax.shard_map(
        local,
        mesh=mesh,
        in_specs=(
            P("seq", None, "tensor"),
            P(None, None, "tensor"),
            P(None, "tensor"),
            P("seq", "tensor"),
            P(None, "tensor"),
            P("seq", "tensor"),
        ),
        out_specs=(
            P("seq", "tensor"),
            P("seq", None, "tensor"),
            P("seq", "tensor"),
            P(None, "tensor"),
            P(None, None, "tensor"),
        ),
        check_vma=False,
    )
```

profile of v0, /device:TPU:0, one launch (start us, length us, event | category | flops | bytes accessed | tf_op | source)
XLA Modules:
  0.0 607.2 jit_solution(8944364279748115227)
XLA Ops:
  8.7 4.9 collective-permute-start
  23.4 11.5 %all-gather.2.cloned.1.call-done = bf16[128,8192]{1,0:T(8,128)(2,1)} async-done(((bf16[128,2048]{1,0:T(8,128)(2,1)}), bf16[128,8192]{1,0:T(8,128)(2,1)}) %all-gather.2.cloned.1.call-update) | async-done | bytes 2097168 | tf_op jit(solution)/shard_map/all_gather | solution.py:157
  34.9 9.8 %slice_multiply_fusion.1 = (f32[128,1024]{1,0:T(8,128)}, f32[128,1024]{1,0:T(8,128)S(1)}, f32[128,1024]{1,0:T(8,128)}) fusion(f32[128,3072]{1,0:T(8,128)S(1)} %slice_bitcast_fusion, bf16[128,8192]{1,0:T(8,128)(2,1)} %all-gather.2.cloned.1.call-done, bf16[8192,1024]{1,0:T(8,128)(2,1)} %param.10), kind=kOutput, calls=%fused_computation.100 | convolution fusion | flops 2147745792 | bytes 22020096 | tf_op jit(solution)/shard_map/dot_general | solution.py:158
  44.7 3.4 collective-permute-start.1
  48.4 4.6 all-to-all-start.4
  55.0 5.3 fusion.57
  61.7 5.9 all-to-all-done.4
  67.6 4.1 all-to-all-start
  74.9 2.6 copy.142
  77.5 20.0 %all-to-all-done = f32[2,8,16,1024]{3,2,0,1:T(8,128)S(1)} async-done(((f32[2,8,16,1024]{3,2,0,1:T(8,128)}), f32[2,8,16,1024]{3,2,0,1:T(8,128)S(1)}, u32[]{:S(2)}, u32[]{:S(2)}) %all-to-all-start) | async-done | bytes 1048608 | tf_op jit(solution)/shard_map/all_to_all | solution.py:50
  97.5 3.6 all-to-all-start.5
  103.5 3.0 fusion.7
  107.1 4.4 copy.127
  111.5 38.0 %all-to-all-done.5 = f32[2,1,16,16,1024]{4,3,1,0,2:T(8,128)S(1)} async-done(((f32[2,1,16,16,1024]{4,3,1,0,2:T(8,128)}), f32[2,1,16,16,1024]{4,3,1,0,2:T(8,128)S(1)}, u32[]{:S(2)}, u32[]{:S(2)}) %all-to-all-start.5) | async-done | bytes 2097184 | tf_op jit(solution)/shard_map/all_to_all | solution.py:72
  149.5 5.0 all-to-all-start.1
  157.3 2.9 fusion.23
  160.2 2.9 fusion.67
  163.1 83.5 %all-to-all-done.1 = f32[2,2,16,16,1024]{4,3,1,0,2:T(8,128)} async-done(((f32[2,2,16,16,1024]{4,3,1,0,2:T(8,128)}), f32[2,2,16,16,1024]{4,3,1,0,2:T(8,128)}, u32[]{:S(2)}, u32[]{:S(2)}) %all-to-all-start.1) | async-done | bytes 4194336 | tf_op jit(solution)/shard_map/all_to_all | solution.py:72
  246.6 2.5 copy.128
  250.0 3.6 fusion.81
  253.8 3.8 fusion.79
  257.6 3.7 add_bitcast_fusion.1
  261.3 3.7 subtract_bitcast_fusion.1
  265.0 2.8 multiply_add_fusion.1
  274.2 2.5 subtract_bitcast_fusion
  279.1 7.3 %copy.150 = f32[2,2,2,128,1024]{4,2,1,0,3:T(2,128)} copy(f32[2,2,2,128,1024]{3,4,2,1,0:T(8,128)} %pad_maximum_fusion.1) | data formatting | bytes 8388608 | tf_op jit(solution)/shard_map/stack | solution.py:100
  286.4 4.6 all-to-all-start.6
  298.7 84.8 %all-to-all-done.6 = f32[2,2,2,128,1024]{4,2,1,0,3:T(2,128)} async-done(((f32[2,2,2,128,1024]{4,2,1,0,3:T(2,128)}), f32[2,2,2,128,1024]{4,2,1,0,3:T(2,128)}, u32[]{:S(2)}, u32[]{:S(2)}) %all-to-all-start.6) | async-done | bytes 4194336 | tf_op jit(solution)/shard_map/all_to_all | solution.py:106
  383.5 3.8 all-to-all-start.2
  387.3 4.6 copy.151
  393.7 3.0 copy.152
  396.7 3.7 squeeze.21
  400.4 4.6 copy.153
  405.0 3.6 squeeze.22
  408.6 3.0 fusion.117
  414.6 21.1 %all-to-all-done.2 = f32[2,1,2,128,1024]{4,2,1,0,3:T(2,128)S(1)} async-done(((f32[2,1,2,128,1024]{4,2,1,0,3:T(2,128)}), f32[2,1,2,128,1024]{4,2,1,0,3:T(2,128)S(1)}, u32[]{:S(2)}, u32[]{:S(2)}) %all-to-all-start.2) | async-done | bytes 2097184 | tf_op jit(solution)/shard_map/all_to_all | solution.py:106
  435.7 3.9 all-to-all-start.7
  443.5 3.0 copy.138
  451.0 14.5 %all-to-all-done.7 = f32[2,8,16,1024]{3,2,0,1:T(8,128)S(1)} async-done(((f32[2,8,16,1024]{3,2,0,1:T(8,128)}), f32[2,8,16,1024]{3,2,0,1:T(8,128)S(1)}, u32[]{:S(2)}, u32[]{:S(2)}) %all-to-all-start.7) | async-done | bytes 1048608 | tf_op jit(solution)/shard_map/all_to_all | solution.py:114
  465.5 3.6 all-to-all-start.3
  471.3 5.3 fusion.51
  476.7 2.6 rev.14
  479.4 3.7 collective-permute-done.2
  484.2 6.2 %fusion.55 = f32[1,128,1024]{2,0,1:T(1,128)} fusion(f32[1,247,1024]{2,0,1:T(1,128)S(1)} %broadcast_in_dim.20, f32[120,1,1024]{2,0,1:T(8,128)S(1)} %bitcast.294), kind=kOutput, calls=%fused_computation.106 | convolution fusion | flops 188743680 | bytes 2027520 | tf_op jit(solution)/shard_map/conv_general_dilated | solution.py:26
  492.9 13.3 %fusion.276 = f32[128,8192]{1,0:T(8,128)} fusion(bf16[128,1024]{1,0:T(8,128)(2,1)S(1)} %get-tuple-element.49, bf16[8192,1024]{1,0:T(8,128)(2,1)} %param.10), kind=kOutput, calls=%fused_computation.310 | convolution fusion | flops 2147483648 | bytes 21233664 | tf_op jit(solution)/shard_map/dot_general | solution.py:151
  508.8 3.7 fusion.14
  514.6 39.4 %psum.15 = bf16[7,3072]{1,0:T(8,128)(2,1)S(1)} all-reduce(bf16[7,3072]{1,0:T(8,128)(2,1)S(1)} %rev.15), channel_id=1, replica_groups=mesh['seq'=8,'tensor'=4] {'seq'}, use_global_device_ids=true, to_apply=%region_2.3 | all-reduce | flops 21504 | bytes 86016 | tf_op jit(solution)/shard_map/psum | solution.py:194
  562.9 35.2 %reduce-scatter.2.cloned.1.call-done = f32[128,2048]{1,0:T(8,128)} async-done(((f32[128,8192]{1,0:T(8,128)}), f32[128,2048]{1,0:T(8,128)}) %reduce-scatter.2.cloned.1.call-update) | async-done | bytes 1048592 | tf_op jit(solution)/shard_map/reduce_scatter | solution.py:154
  (140 shorter events, 75.5 us)
Async XLA Ops:
  7.2 8.0 %copy-start.15 = (f32[7,3,1024]{2,0,1:T(8,128)S(1)}, f32[7,3,1024]{2,0,1:T(8,128)}, u32[]{:S(2)}) copy-start(f32[7,3,1024]{2,0,1:T(8,128)} %param.7) | copy-start | bytes 258052
  7.2 27.7 %all-gather.2.cloned.1.call-start = ((), (), s32[]{:S(2)}) async-start(), calls=%async_computation.10 | async-start | bytes 2621440 | tf_op jit(solution)/shard_map/all_gather | solution.py:157
  8.7 7.1 %collective-permute-start = (bf16[6,3072]{1,0:T(8,128)(2,1)S(1)}, bf16[6,3072]{1,0:T(8,128)(2,1)S(1)}, u32[]{:S(2)}, u32[]{:S(2)}) collective-permute-start(bf16[6,3072]{1,0:T(8,128)(2,1)S(1)} %bitcast.300), channel_id=1, source_target_pairs={{0,4},{4,8},{8,12},{12,16},{16,20},{20,24},{24,28},{1,5},{5,9},{9,... | collective-permute-start | bytes 110600 | tf_op jit(solution)/shard_map/ppermute | solution.py:13
  17.5 0.9 copy-start.7
  17.6 0.9 copy-start.17
  23.4 21.3 %copy-start = (f32[128,3072]{1,0:T(8,128)}, f32[128,3072]{1,0:T(8,128)S(1)}, u32[]{:S(2)}) copy-start(f32[128,3072]{1,0:T(8,128)S(1)} %slice_bitcast_fusion) | copy-start | bytes 4718596
  23.4 24.7 %copy-start.13 = (f32[120,1024]{1,0:T(8,128)S(1)}, f32[120,1024]{1,0:T(8,128)}, u32[]{:S(2)}) copy-start(f32[120,1024]{1,0:T(8,128)} %param.8) | copy-start | bytes 1474564
  44.7 9.4 %collective-permute-start.1 = (bf16[119,1024]{1,0:T(8,128)(2,1)S(1)}, bf16[119,1024]{1,0:T(8,128)(2,1)S(1)}, u32[]{:S(2)}, u32[]{:S(2)}) collective-permute-start(bf16[119,1024]{1,0:T(8,128)(2,1)S(1)} %slice.165), channel_id=1, source_target_pairs={{0,4},{4,8},{8,12},{12,16},{16,20},{20,24},{24,28},{1,5},{5,9},{9,... | collective-permute-start | bytes 731144 | tf_op jit(solution)/shard_map/ppermute | solution.py:13
  48.4 19.2 %all-to-all-start.4 = ((f32[1,8,16,1024]{3,2,0,1:T(8,128)}), f32[1,8,16,1024]{3,2,0,1:T(8,128)S(1)}, u32[]{:S(2)}, u32[]{:S(2)}) async-start(f32[1,8,16,1024]{3,2,0,1:T(8,128)} %bitcast.49), calls=%async_computation.5 | async-start | bytes 1048576 | tf_op jit(solution)/shard_map/all_to_all | solution.py:50
  54.9 5.4 copy-start.10
  55.0 5.5 copy-start.12
  67.6 29.9 %all-to-all-start = ((f32[2,8,16,1024]{3,2,0,1:T(8,128)}), f32[2,8,16,1024]{3,2,0,1:T(8,128)S(1)}, u32[]{:S(2)}, u32[]{:S(2)}) async-start(f32[2,8,16,1024]{3,2,0,1:T(8,128)} %copy.124), calls=%async_computation | async-start | bytes 2097152 | tf_op jit(solution)/shard_map/all_to_all | solution.py:50
  97.5 52.1 %all-to-all-start.5 = ((f32[2,1,16,16,1024]{4,3,1,0,2:T(8,128)}), f32[2,1,16,16,1024]{4,3,1,0,2:T(8,128)S(1)}, u32[]{:S(2)}, u32[]{:S(2)}) async-start(f32[2,1,16,16,1024]{4,3,1,0,2:T(8,128)} %copy.142), calls=%async_computation.6 | async-start | bytes 4194304 | tf_op jit(solution)/shard_map/all_to_all | solution.py:72
  149.5 97.1 %all-to-all-start.1 = ((f32[2,2,16,16,1024]{4,3,1,0,2:T(8,128)}), f32[2,2,16,16,1024]{4,3,1,0,2:T(8,128)}, u32[]{:S(2)}, u32[]{:S(2)}) async-start(f32[2,2,16,16,1024]{4,3,1,0,2:T(8,128)} %copy.127), calls=%async_computation.1 | async-start | bytes 8388608 | tf_op jit(solution)/shard_map/all_to_all | solution.py:72
  261.2 3.7 copy-start.5
  261.2 3.7 copy-start.6
  286.4 97.1 %all-to-all-start.6 = ((f32[2,2,2,128,1024]{4,2,1,0,3:T(2,128)}), f32[2,2,2,128,1024]{4,2,1,0,3:T(2,128)}, u32[]{:S(2)}, u32[]{:S(2)}) async-start(f32[2,2,2,128,1024]{4,2,1,0,3:T(2,128)} %copy.150), calls=%async_computation.7 | async-start | bytes 8388608 | tf_op jit(solution)/shard_map/all_to_all | solution.py:106
  383.5 52.2 %all-to-all-start.2 = ((f32[2,1,2,128,1024]{4,2,1,0,3:T(2,128)}), f32[2,1,2,128,1024]{4,2,1,0,3:T(2,128)S(1)}, u32[]{:S(2)}, u32[]{:S(2)}) async-start(f32[2,1,2,128,1024]{4,2,1,0,3:T(2,128)} %copy.135), calls=%async_computation.2 | async-start | bytes 4194304 | tf_op jit(solution)/shard_map/all_to_all | solution.py:106
  408.6 3.0 copy-start.2
  435.7 29.8 %all-to-all-start.7 = ((f32[2,8,16,1024]{3,2,0,1:T(8,128)}), f32[2,8,16,1024]{3,2,0,1:T(8,128)S(1)}, u32[]{:S(2)}, u32[]{:S(2)}) async-start(f32[2,8,16,1024]{3,2,0,1:T(8,128)} %copy.154), calls=%async_computation.8 | async-start | bytes 2097152 | tf_op jit(solution)/shard_map/all_to_all | solution.py:114
  449.9 21.3 %copy-start.11 = (f32[1,247,1024]{2,0,1:T(1,128)S(1)}, f32[1,247,1024]{2,0,1:T(1,128)}, u32[]{:S(2)}) copy-start(f32[1,247,1024]{2,0,1:T(1,128)} %copy-done.10) | copy-start | bytes 3035140
  465.5 11.1 %copy-start.3 = (f32[2,8,16,1024]{3,2,0,1:T(8,128)}, f32[2,8,16,1024]{3,2,0,1:T(8,128)S(1)}, u32[]{:S(2)}) copy-start(f32[2,8,16,1024]{3,2,0,1:T(8,128)S(1)} %all-to-all-done.7) | copy-start | bytes 3145732
  465.5 24.9 %all-to-all-start.3 = ((f32[1,8,16,1024]{3,2,0,1:T(8,128)}), f32[1,8,16,1024]{3,2,0,1:T(8,128)S(1)}, u32[]{:S(2)}, u32[]{:S(2)}) async-start(f32[1,8,16,1024]{3,2,0,1:T(8,128)} %copy.139), calls=%async_computation.3 | async-start | bytes 1048576 | tf_op jit(solution)/shard_map/all_to_all | solution.py:114
  469.1 85.5 %all-reduce.2.cloned.1.call-start = ((), (), s32[]{:S(2)}) async-start(), calls=%async_computation.11 | async-start | bytes 491520 | tf_op jit(solution)/shard_map/psum | solution.py:193
  470.0 13.1 %collective-permute-start.2 = (bf16[119,1024]{1,0:T(8,128)(2,1)}, bf16[119,1024]{1,0:T(8,128)(2,1)S(1)}, u32[]{:S(2)}, u32[]{:S(2)}) collective-permute-start(bf16[119,1024]{1,0:T(8,128)(2,1)} %slice.164), channel_id=1, source_target_pairs={{4,0},{8,4},{12,8},{16,12},{20,16},{24,20},{28,24},{5,1},{9,5},{13... | collective-permute-start | bytes 731144 | tf_op jit(solution)/shard_map/ppermute | solution.py:13
  479.3 118.9 %reduce-scatter.2.cloned.1.call-start = ((), (), s32[]{:S(2)}) async-start(), calls=%async_computation.9 | async-start | bytes 5242880 | tf_op jit(solution)/shard_map/reduce_scatter | solution.py:154
  483.1 1.0 copy-start.14
  484.2 7.0 %copy-start.1 = (f32[128,3072]{1,0:T(8,128)S(1)}, f32[128,3072]{1,0:T(8,128)}, u32[]{:S(2)}) copy-start(f32[128,3072]{1,0:T(8,128)} %copy-done) | copy-start | bytes 4718596
  490.4 0.8 copy-start.9
  506.2 1.2 copy-start.4
  507.4 1.3 copy-start.8
  513.3 43.2 %collective-permute-start.3 = (bf16[6,3072]{1,0:T(8,128)(2,1)S(1)}, bf16[6,3072]{1,0:T(8,128)(2,1)S(1)}, u32[]{:S(2)}, u32[]{:S(2)}) collective-permute-start(bf16[6,3072]{1,0:T(8,128)(2,1)S(1)} %slice.166), channel_id=1, source_target_pairs={{4,0},{8,4},{12,8},{16,12},{20,16},{24,20},{28,24},{5,1},{9,5},{13... | collective-permute-start | bytes 110600 | tf_op jit(solution)/shard_map/ppermute | solution.py:13
  558.7 0.9 copy-start.16
  558.7 0.9 copy-start.18
Sparse Core Ops, SparseCore 0:
  9.5 25.2 all-gather.1
  479.4 72.5 all-reduce.1
  554.6 43.5 reduce-scatter.1
where the time goes:
time: 616 us; the launch traced here: 607 us
  waiting for transfers between devices  320 us (52%)
  matrix products  98.7 us (16%)
  local copies, waits for them, and re-layouts  77.8 us (13%)
  starting transfers between devices  44.2 us (7%)
  blocking collectives  39.4 us (6%)
  between operations  15.1 us (2%)
  other arithmetic  11.9 us (2%)
    all_to_all x2, waiting for transfers between devices, to_spectrum(): lax.all_to_all(turned, 'seq', split_axis=2, concat_axis=3, tiled=True)  122 us
    all_to_all x2, waiting for transfers between devices, from_spectrum(): lax.all_to_all(turned, 'seq', split_axis=3, concat_axis=2, tiled=True)  106 us
    psum x1, blocking collectives, local(): lax.psum(short_part.astype(jnp.bfloat16), 'seq').astype(jnp.float32)  39.4 us
    reduce_scatter x1, waiting for transfers between devices, local(): lax.psum_scatter(partial_out, 'tensor', scatter_dimension=1, tiled=True)  35.2 us
    all_to_all x2, waiting for transfers between devices, to_spectrum(): lax.all_to_all(signals.reshape(signal_count, devices, stride, channels),...  25.9 us
    conv_general_dilated x6, matrix products, correlate(): lax.conv_general_dilated(signal[None], kernel[:, None, :], (1,), 'VALID',...  22.3 us
    all_to_all x2, waiting for transfers between devices, from_spectrum(): lax.all_to_all(blocks, 'seq', split_axis=1, concat_axis=1, tiled=True)  14.5 us
    dot_general x1, matrix products, local(): lax.dot_general(product, out_weight, (((1,), (1,)), ((), ())), preferred_...  13.3 us
  transfers between devices with their start and end apart: 15, of which 11 were waited for; matrix products, arithmetic and copies ran while one was open for 22% of the time, Pallas kernels for 0%

commit v1 on v0

--- a/solution.py
+++ b/solution.py
@@ -69,7 +69,10 @@
             first_imag * cosine_values - first_real * sine_part,
         ]
     )
-    arrived = lax.all_to_all(turned, "seq", split_axis=2, concat_axis=3, tiled=True)
+    arrived = jnp.concatenate(
+        lax.all_to_all(jnp.stack(jnp.split(turned, lax.axis_size("seq"), axis=2)), "seq", 0, 0),
+        axis=3,
+    )
     spec_real = jnp.einsum("km,sjmc->sjkc", cos_table, arrived[0], precision=precise) + jnp.einsum(
         "km,sjmc->sjkc", sin_table, arrived[1], precision=precise
     )

time: 616 us -> 617 us (level)
  other arithmetic: 11.9 us -> 19.9 us
    unnamed x0 -> x7, other arithmetic: none -> 7.27 us
  transfers between devices with their start and end apart: 15 -> 15, of which waited for: 11 -> 11; matrix products, arithmetic and copies ran while one was open for 22% -> 23% of each run, Pallas kernels for 0% -> 0%
where the time goes in v1:
time: 617 us; the launch traced here: 608 us
  waiting for transfers between devices  316 us (51%)
  matrix products  96.1 us (16%)
  local copies, waits for them, and re-layouts  78.5 us (13%)
  starting transfers between devices  43.6 us (7%)
  blocking collectives  39.4 us (6%)
  other arithmetic  19.9 us (3%)
  between operations  15.2 us (2%)
    all_to_all x2, waiting for transfers between devices, to_spectrum(): lax.all_to_all(jnp.stack(jnp.split(turned, lax.axis_size('seq'), axis=2))...  116 us
    all_to_all x2, waiting for transfers between devices, from_spectrum(): lax.all_to_all(turned, 'seq', split_axis=3, concat_axis=2, tiled=True)  106 us
    psum x1, blocking collectives, local(): lax.psum(short_part.astype(jnp.bfloat16), 'seq').astype(jnp.float32)  39.4 us
    reduce_scatter x1, waiting for transfers between devices, local(): lax.psum_scatter(partial_out, 'tensor', scatter_dimension=1, tiled=True)  35.3 us
    all_to_all x2, waiting for transfers between devices, to_spectrum(): lax.all_to_all(signals.reshape(signal_count, devices, stride, channels),...  26.7 us
    conv_general_dilated x6, matrix products, correlate(): lax.conv_general_dilated(signal[None], kernel[:, None, :], (1,), 'VALID',...  22.3 us
    all_to_all x2, waiting for transfers between devices, from_spectrum(): lax.all_to_all(blocks, 'seq', split_axis=1, concat_axis=1, tiled=True)  14.5 us
    dot_general x1, matrix products, local(): lax.dot_general(product, out_weight, (((1,), (1,)), ((), ())), preferred_...  13.4 us
  transfers between devices with their start and end apart: 15, of which 11 were waited for; matrix products, arithmetic and copies ran while one was open for 23% of the time, Pallas kernels for 0%

profile of v1, /device:TPU:0, one launch (start us, length us, event | category | flops | bytes accessed | tf_op | source)
XLA Modules:
  0.0 608.2 jit_solution(10297950714115146025)
XLA Ops:
  8.7 4.9 collective-permute-start
  23.4 11.4 %all-gather.2.cloned.1.call-done = bf16[128,8192]{1,0:T(8,128)(2,1)} async-done(((bf16[128,2048]{1,0:T(8,128)(2,1)}), bf16[128,8192]{1,0:T(8,128)(2,1)}) %all-gather.2.cloned.1.call-update) | async-done | bytes 2097168 | tf_op jit(solution)/shard_map/all_gather | solution.py:160
  34.9 9.8 %slice_multiply_fusion.1 = (f32[128,1024]{1,0:T(8,128)}, f32[128,1024]{1,0:T(8,128)S(1)}, f32[128,1024]{1,0:T(8,128)}) fusion(f32[128,3072]{1,0:T(8,128)S(1)} %slice_bitcast_fusion, bf16[128,8192]{1,0:T(8,128)(2,1)} %all-gather.2.cloned.1.call-done, bf16[8192,1024]{1,0:T(8,128)(2,1)} %param.10), kind=kOutput, calls=%fused_computation.140 | convolution fusion | flops 2147745792 | bytes 22020096 | tf_op jit(solution)/shard_map/dot_general | solution.py:161
  44.7 3.4 collective-permute-start.1
  48.5 4.6 all-to-all-start.4
  54.8 5.3 fusion.81
  61.5 6.2 %all-to-all-done.4 = f32[1,8,16,1024]{3,2,0,1:T(8,128)S(1)} async-done(((f32[1,8,16,1024]{3,2,0,1:T(8,128)}), f32[1,8,16,1024]{3,2,0,1:T(8,128)S(1)}, u32[]{:S(2)}, u32[]{:S(2)}) %all-to-all-start.4) | async-done | bytes 524320 | tf_op jit(solution)/shard_map/all_to_all | solution.py:50
  67.7 3.9 all-to-all-start
  77.1 20.5 %all-to-all-done = f32[2,8,16,1024]{3,2,0,1:T(8,128)S(1)} async-done(((f32[2,8,16,1024]{3,2,0,1:T(8,128)}), f32[2,8,16,1024]{3,2,0,1:T(8,128)S(1)}, u32[]{:S(2)}, u32[]{:S(2)}) %all-to-all-start) | async-done | bytes 1048608 | tf_op jit(solution)/shard_map/all_to_all | solution.py:50
  97.6 3.6 all-to-all-start.5
  101.2 2.4 fusion.43
  103.7 3.1 fusion.10
  115.2 34.4 %all-to-all-done.5 = f32[8,2,1,2,16,1024]{5,3,4,1,2,0:T(2,128)S(1)} async-done(((f32[8,2,1,2,16,1024]{5,3,4,1,2,0:T(2,128)}), f32[8,2,1,2,16,1024]{5,3,4,1,2,0:T(2,128)S(1)}, u32[]{:S(2)}, u32[]{:S(2)}) %all-to-all-start.5) | async-done | bytes 2097184 | tf_op jit(solution)/shard_map/all_to_all | solution.py:73
  149.6 4.6 all-to-all-start.1
  154.3 2.2 fusion.294
  164.7 82.1 %all-to-all-done.1 = f32[8,2,2,2,16,1024]{5,3,4,2,1,0:T(2,128)} async-done(((f32[8,2,2,2,16,1024]{5,3,4,2,1,0:T(2,128)}), f32[8,2,2,2,16,1024]{5,3,4,2,1,0:T(2,128)}, u32[]{:S(2)}, u32[]{:S(2)}) %all-to-all-start.1) | async-done | bytes 4194336 | tf_op jit(solution)/shard_map/all_to_all | solution.py:73
  246.7 3.8 fusion.293
  251.1 3.6 fusion.115
  255.4 3.8 fusion.113
  259.1 3.7 add_bitcast_fusion.1
  262.8 3.7 subtract_bitcast_fusion.1
  268.4 2.5 fusion.11
  275.2 2.5 subtract_bitcast_fusion
  277.7 2.3 pad_maximum_fusion
  280.0 7.3 %copy.119 = f32[2,2,2,128,1024]{4,2,1,0,3:T(2,128)} copy(f32[2,2,2,128,1024]{3,4,2,1,0:T(8,128)} %pad_maximum_fusion) | data formatting | bytes 8388608 | tf_op jit(solution)/shard_map/stack | solution.py:103
  287.3 4.5 all-to-all-start.6
  297.1 2.5 copy.101
  299.6 84.9 %all-to-all-done.6 = f32[2,2,2,128,1024]{4,2,1,0,3:T(2,128)} async-done(((f32[2,2,2,128,1024]{4,2,1,0,3:T(2,128)}), f32[2,2,2,128,1024]{4,2,1,0,3:T(2,128)}, u32[]{:S(2)}, u32[]{:S(2)}) %all-to-all-start.6) | async-done | bytes 4194336 | tf_op jit(solution)/shard_map/all_to_all | solution.py:109
  384.5 3.8 all-to-all-start.2
  388.3 4.6 copy.120
  394.7 3.0 copy.121
  397.7 3.6 squeeze.21
  401.3 4.6 copy.122
  405.9 3.6 squeeze.22
  409.6 3.0 fusion.151
  415.6 21.1 %all-to-all-done.2 = f32[2,1,2,128,1024]{4,2,1,0,3:T(2,128)S(1)} async-done(((f32[2,1,2,128,1024]{4,2,1,0,3:T(2,128)}), f32[2,1,2,128,1024]{4,2,1,0,3:T(2,128)S(1)}, u32[]{:S(2)}, u32[]{:S(2)}) %all-to-all-start.2) | async-done | bytes 2097184 | tf_op jit(solution)/shard_map/all_to_all | solution.py:109
  436.7 3.9 all-to-all-start.7
  444.5 3.0 copy.104
  452.0 14.5 %all-to-all-done.7 = f32[2,8,16,1024]{3,2,0,1:T(8,128)S(1)} async-done(((f32[2,8,16,1024]{3,2,0,1:T(8,128)}), f32[2,8,16,1024]{3,2,0,1:T(8,128)S(1)}, u32[]{:S(2)}, u32[]{:S(2)}) %all-to-all-start.7) | async-done | bytes 1048608 | tf_op jit(solution)/shard_map/all_to_all | solution.py:117
  466.4 3.6 all-to-all-start.3
  472.2 5.3 fusion.75
  477.6 2.6 rev.14
  480.3 3.7 collective-permute-done.2
  485.1 6.2 %fusion.79 = f32[1,128,1024]{2,0,1:T(1,128)} fusion(f32[1,247,1024]{2,0,1:T(1,128)S(1)} %broadcast_in_dim.20, f32[120,1,1024]{2,0,1:T(8,128)S(1)} %bitcast.359), kind=kOutput, calls=%fused_computation.146 | convolution fusion | flops 188743680 | bytes 2027520 | tf_op jit(solution)/shard_map/conv_general_dilated | solution.py:26
  493.8 13.4 %fusion.310 = f32[128,8192]{1,0:T(8,128)} fusion(bf16[128,1024]{1,0:T(8,128)(2,1)S(1)} %get-tuple-element.44, bf16[8192,1024]{1,0:T(8,128)(2,1)} %param.10), kind=kOutput, calls=%fused_computation.367 | convolution fusion | flops 2147483648 | bytes 21233664 | tf_op jit(solution)/shard_map/dot_general | solution.py:154
  509.8 3.7 fusion.15
  515.6 39.4 %psum.15 = bf16[7,3072]{1,0:T(8,128)(2,1)S(1)} all-reduce(bf16[7,3072]{1,0:T(8,128)(2,1)S(1)} %rev.15), channel_id=1, replica_groups=mesh['seq'=8,'tensor'=4] {'seq'}, use_global_device_ids=true, to_apply=%region_2.3 | all-reduce | flops 21504 | bytes 86016 | tf_op jit(solution)/shard_map/psum | solution.py:197
  563.8 35.3 %reduce-scatter.2.cloned.1.call-done = f32[128,2048]{1,0:T(8,128)} async-done(((f32[128,8192]{1,0:T(8,128)}), f32[128,2048]{1,0:T(8,128)}) %reduce-scatter.2.cloned.1.call-update) | async-done | bytes 1048592 | tf_op jit(solution)/shard_map/reduce_scatter | solution.py:157
  (155 shorter events, 83.6 us)
Async XLA Ops:
  7.2 8.0 %copy-start.17 = (f32[7,3,1024]{2,0,1:T(8,128)S(1)}, f32[7,3,1024]{2,0,1:T(8,128)}, u32[]{:S(2)}) copy-start(f32[7,3,1024]{2,0,1:T(8,128)} %param.7) | copy-start | bytes 258052
  7.2 27.7 %all-gather.2.cloned.1.call-start = ((), (), s32[]{:S(2)}) async-start(), calls=%async_computation.10 | async-start | bytes 2621440 | tf_op jit(solution)/shard_map/all_gather | solution.py:160
  8.7 7.1 %collective-permute-start = (bf16[6,3072]{1,0:T(8,128)(2,1)S(1)}, bf16[6,3072]{1,0:T(8,128)(2,1)S(1)}, u32[]{:S(2)}, u32[]{:S(2)}) collective-permute-start(bf16[6,3072]{1,0:T(8,128)(2,1)S(1)} %bitcast.365), channel_id=1, source_target_pairs={{0,4},{4,8},{8,12},{12,16},{16,20},{20,24},{24,28},{1,5},{5,9},{9,... | collective-permute-start | bytes 110600 | tf_op jit(solution)/shard_map/ppermute | solution.py:13
  17.6 0.9 copy-start.8
  17.6 0.9 copy-start.19
  23.4 21.2 %copy-start = (f32[128,3072]{1,0:T(8,128)}, f32[128,3072]{1,0:T(8,128)S(1)}, u32[]{:S(2)}) copy-start(f32[128,3072]{1,0:T(8,128)S(1)} %slice_bitcast_fusion) | copy-start | bytes 4718596
  23.4 24.7 %copy-start.15 = (f32[120,1024]{1,0:T(8,128)S(1)}, f32[120,1024]{1,0:T(8,128)}, u32[]{:S(2)}) copy-start(f32[120,1024]{1,0:T(8,128)} %param.8) | copy-start | bytes 1474564
  44.7 9.3 %collective-permute-start.1 = (bf16[119,1024]{1,0:T(8,128)(2,1)S(1)}, bf16[119,1024]{1,0:T(8,128)(2,1)S(1)}, u32[]{:S(2)}, u32[]{:S(2)}) collective-permute-start(bf16[119,1024]{1,0:T(8,128)(2,1)S(1)} %slice.165), channel_id=1, source_target_pairs={{0,4},{4,8},{8,12},{12,16},{16,20},{20,24},{24,28},{1,5},{5,9},{9,... | collective-permute-start | bytes 731144 | tf_op jit(solution)/shard_map/ppermute | solution.py:13
  48.5 19.2 %all-to-all-start.4 = ((f32[1,8,16,1024]{3,2,0,1:T(8,128)}), f32[1,8,16,1024]{3,2,0,1:T(8,128)S(1)}, u32[]{:S(2)}, u32[]{:S(2)}) async-start(f32[1,8,16,1024]{3,2,0,1:T(8,128)} %bitcast.55), calls=%async_computation.5 | async-start | bytes 1048576 | tf_op jit(solution)/shard_map/all_to_all | solution.py:50
  54.8 5.4 copy-start.12
  54.8 5.5 copy-start.14
  67.7 29.9 %all-to-all-start = ((f32[2,8,16,1024]{3,2,0,1:T(8,128)}), f32[2,8,16,1024]{3,2,0,1:T(8,128)S(1)}, u32[]{:S(2)}, u32[]{:S(2)}) async-start(f32[2,8,16,1024]{3,2,0,1:T(8,128)} %copy.92), calls=%async_computation | async-start | bytes 2097152 | tf_op jit(solution)/shard_map/all_to_all | solution.py:50
  75.8 1.3 copy-start.10
  97.6 52.1 %all-to-all-start.5 = ((f32[8,2,1,2,16,1024]{5,3,4,1,2,0:T(2,128)}), f32[8,2,1,2,16,1024]{5,3,4,1,2,0:T(2,128)S(1)}, u32[]{:S(2)}, u32[]{:S(2)}) async-start(f32[8,2,1,2,16,1024]{5,3,4,1,2,0:T(2,128)} %copy-done.10), calls=%async_computation.6 | async-start | bytes 4194304 | tf_op jit(solution)/shard_map/all_to_all | solution.py:73
  149.6 97.1 %all-to-all-start.1 = ((f32[8,2,2,2,16,1024]{5,3,4,2,1,0:T(2,128)}), f32[8,2,2,2,16,1024]{5,3,4,2,1,0:T(2,128)}, u32[]{:S(2)}, u32[]{:S(2)}) async-start(f32[8,2,2,2,16,1024]{5,3,4,2,1,0:T(2,128)} %fusion.71), calls=%async_computation.1 | async-start | bytes 8388608 | tf_op jit(solution)/shard_map/all_to_all | solution.py:73
  156.5 1.6 copy-start.5
  262.8 3.7 copy-start.6
  262.8 3.7 copy-start.7
  287.3 97.1 %all-to-all-start.6 = ((f32[2,2,2,128,1024]{4,2,1,0,3:T(2,128)}), f32[2,2,2,128,1024]{4,2,1,0,3:T(2,128)}, u32[]{:S(2)}, u32[]{:S(2)}) async-start(f32[2,2,2,128,1024]{4,2,1,0,3:T(2,128)} %copy.119), calls=%async_computation.7 | async-start | bytes 8388608 | tf_op jit(solution)/shard_map/all_to_all | solution.py:109
  384.5 52.2 %all-to-all-start.2 = ((f32[2,1,2,128,1024]{4,2,1,0,3:T(2,128)}), f32[2,1,2,128,1024]{4,2,1,0,3:T(2,128)S(1)}, u32[]{:S(2)}, u32[]{:S(2)}) async-start(f32[2,1,2,128,1024]{4,2,1,0,3:T(2,128)} %copy.101), calls=%async_computation.2 | async-start | bytes 4194304 | tf_op jit(solution)/shard_map/all_to_all | solution.py:109
  409.6 3.0 copy-start.2
  436.7 29.8 %all-to-all-start.7 = ((f32[2,8,16,1024]{3,2,0,1:T(8,128)}), f32[2,8,16,1024]{3,2,0,1:T(8,128)S(1)}, u32[]{:S(2)}, u32[]{:S(2)}) async-start(f32[2,8,16,1024]{3,2,0,1:T(8,128)} %copy.123), calls=%async_computation.8 | async-start | bytes 2097152 | tf_op jit(solution)/shard_map/all_to_all | solution.py:117
  450.8 21.4 %copy-start.13 = (f32[1,247,1024]{2,0,1:T(1,128)S(1)}, f32[1,247,1024]{2,0,1:T(1,128)}, u32[]{:S(2)}) copy-start(f32[1,247,1024]{2,0,1:T(1,128)} %copy-done.12) | copy-start | bytes 3035140
  466.4 11.1 %copy-start.3 = (f32[2,8,16,1024]{3,2,0,1:T(8,128)}, f32[2,8,16,1024]{3,2,0,1:T(8,128)S(1)}, u32[]{:S(2)}) copy-start(f32[2,8,16,1024]{3,2,0,1:T(8,128)S(1)} %all-to-all-done.7) | copy-start | bytes 3145732
  466.4 24.9 %all-to-all-start.3 = ((f32[1,8,16,1024]{3,2,0,1:T(8,128)}), f32[1,8,16,1024]{3,2,0,1:T(8,128)S(1)}, u32[]{:S(2)}, u32[]{:S(2)}) async-start(f32[1,8,16,1024]{3,2,0,1:T(8,128)} %copy.105), calls=%async_computation.3 | async-start | bytes 1048576 | tf_op jit(solution)/shard_map/all_to_all | solution.py:117
  470.1 85.5 %all-reduce.2.cloned.1.call-start = ((), (), s32[]{:S(2)}) async-start(), calls=%async_computation.11 | async-start | bytes 491520 | tf_op jit(solution)/shard_map/psum | solution.py:196
  470.9 13.1 %collective-permute-start.2 = (bf16[119,1024]{1,0:T(8,128)(2,1)}, bf16[119,1024]{1,0:T(8,128)(2,1)S(1)}, u32[]{:S(2)}, u32[]{:S(2)}) collective-permute-start(bf16[119,1024]{1,0:T(8,128)(2,1)} %slice.164), channel_id=1, source_target_pairs={{4,0},{8,4},{12,8},{16,12},{20,16},{24,20},{28,24},{5,1},{9,5},{13... | collective-permute-start | bytes 731144 | tf_op jit(solution)/shard_map/ppermute | solution.py:13
  480.3 118.9 %reduce-scatter.2.cloned.1.call-start = ((), (), s32[]{:S(2)}) async-start(), calls=%async_computation.9 | async-start | bytes 5242880 | tf_op jit(solution)/shard_map/reduce_scatter | solution.py:157
  484.1 1.0 copy-start.16
  485.1 7.0 %copy-start.1 = (f32[128,3072]{1,0:T(8,128)S(1)}, f32[128,3072]{1,0:T(8,128)}, u32[]{:S(2)}) copy-start(f32[128,3072]{1,0:T(8,128)} %copy-done) | copy-start | bytes 4718596
  491.3 0.8 copy-start.11
  507.2 1.2 copy-start.4
  508.4 1.3 copy-start.9
  514.3 43.1 %collective-permute-start.3 = (bf16[6,3072]{1,0:T(8,128)(2,1)S(1)}, bf16[6,3072]{1,0:T(8,128)(2,1)S(1)}, u32[]{:S(2)}, u32[]{:S(2)}) collective-permute-start(bf16[6,3072]{1,0:T(8,128)(2,1)S(1)} %slice.166), channel_id=1, source_target_pairs={{4,0},{8,4},{12,8},{16,12},{20,16},{24,20},{28,24},{5,1},{9,5},{13... | collective-permute-start | bytes 110600 | tf_op jit(solution)/shard_map/ppermute | solution.py:13
  559.6 0.9 copy-start.18
  559.7 0.9 copy-start.20
Sparse Core Ops, SparseCore 0:
  9.5 25.2 all-gather.1
  480.4 72.5 all-reduce.1
  555.6 43.5 reduce-scatter.1
